TPU v7x, 256 devices: a whole 4x4x8 slice. The times are simulated.
256 devices in a mesh: row: 8 (over z), col: 32 (over y, x, core).
Axes of the slice: x: 4, y: 4, z: 8, core: 2. Of those that a mesh axis runs over, the one named last changes fastest.
Arguments:
- factor: bfloat16 [32, 8, 8, 32, 128, 128], P(None, 'row', None, 'col'), may hold values from -0.046875 to 0.046875
- pattern: int32 [32, 8, 8, 32], P(None, 'row', None, 'col'), may hold values 0 or 1
- loads: float32 [8, 32, 128, 256], P(None, 'col'), may hold values from -6 to 6
- block_inverse: float32 [8, 32, 128, 128], P(None, 'col'), may hold values from -1 to 2, as said below
Outputs:
- solution: float32 [8, 32, 128, 256], P(None, 'col')
Inputs may be any that keep to these rules, and one draw needn't show every extreme that they name: `block_inverse`: each block is lower triangular with diagonal entries between 0.5 and 1.5.
All inputs are finite; a program needn't handle non-finite values. No bound on the sum of `pattern` on one device may be relied on, other than what follows from the above.
Results may differ from a plain program's by a relative error of at most 0.0045.
Values may be sent and summed in bfloat16 or wider, within the bound.
No kernel may reach another device: no remote copies, remote signals or barrier semaphores. Data moves between devices by JAX's collectives and lax.ppermute only.
A program may use at most 128 MiB of HBM per device.

v0:
```python
import jax
import jax.numpy as jnp
from jax import lax
from jax.sharding import PartitionSpec as P

LEVELS = 8


def spread(value, axis, source):
    kept = jnp.where(lax.axis_index(axis) == source, value, 0).astype(value.dtype)
    return lax.psum(kept, axis)


def per_device(factor, pattern, loads, block_inverse):
    row_count = lax.axis_size("row")
    col_count = lax.axis_size("col")
    groups = col_count // row_count
    my_row = lax.axis_index("row")
    my_col = lax.axis_index("col")
    masked = factor[:, 0, :, 0] * pattern[:, 0, :, 0].astype(jnp.bfloat16)[:, :, None, None]
    per_row = factor.shape[0] // LEVELS
    per_col = factor.shape[2] // LEVELS
    rhs_local = loads[:, 0]
    inverse_local = block_inverse[:, 0]
    forward_vals = []
    forward_low = []
    for level_id in range(LEVELS):
        rhs_level = rhs_local[level_id * per_col : (level_id + 1) * per_col]
        inverse_level = inverse_local[level_id * per_col : (level_id + 1) * per_col]
        if level_id > 0:
            panel = masked[level_id * per_row : (level_id + 1) * per_row, : level_id * per_col]
            earlier = jnp.concatenate(forward_low, axis=0)
            partial_sum = jnp.einsum(
                "abpq,bqs->aps", panel, earlier, preferred_element_type=jnp.float32
            )
            row_total = lax.psum(partial_sum, "col")
            row_total = row_total.reshape((per_col, groups) + row_total.shape[1:])
            own_total = lax.dynamic_index_in_dim(
                row_total, my_col // row_count, axis=1, keepdims=False
            )
            solved = jnp.einsum(
                "mpq,mqs->mps",
                inverse_level,
                rhs_level - own_total,
                precision=lax.Precision.HIGHEST,
            )
            solved = spread(solved, "row", my_col % row_count)
        else:
            solved = jnp.einsum(
                "mpq,mqs->mps", inverse_level, rhs_level, precision=lax.Precision.HIGHEST
            )
        forward_vals.append(solved)
        forward_low.append(solved.astype(jnp.bfloat16))
    solution_parts = [None] * LEVELS
    later = []
    for level_id in reversed(range(LEVELS)):
        inverse_level = inverse_local[level_id * per_col : (level_id + 1) * per_col]
        resid = forward_vals[level_id]
        if level_id < LEVELS - 1:
            panel = masked[
                (level_id + 1) * per_row :, level_id * per_col : (level_id + 1) * per_col
            ]
            after = jnp.concatenate(later, axis=0)
            partial_sum = jnp.einsum(
                "abpq,aps->bqs", panel, after, preferred_element_type=jnp.float32
            )
            resid = resid - lax.psum(partial_sum, "row")
        solved = jnp.einsum("mqp,mqs->mps", inverse_level, resid, precision=lax.Precision.HIGHEST)
        solution_parts[level_id] = solved
        if level_id > 0:
            low_solved = solved.astype(jnp.bfloat16)
            pieces = lax.all_gather(low_solved[None], "col", axis=0, tiled=True)
            pieces = pieces.reshape((groups, row_count) + low_solved.shape)
            picked = lax.dynamic_index_in_dim(pieces, my_row, axis=1, keepdims=False)
            arranged = jnp.swapaxes(picked, 0, 1).reshape((per_row,) + low_solved.shape[1:])
            later = [arranged] + later
    solution = jnp.concatenate(solution_parts, axis=0)
    return solution[:, None]


def solution(mesh):
    in_specs = (
        P(None, "row", None, "col", None, None),
        P(None, "row", None, "col"),
        P(None, "col", None, None),
        P(None, "col", None, None),
    )
    out_specs = P(None, "col", None, None)
    return jax.shard_map(
        per_device, mesh=mesh, in_specs=in_specs, out_specs=out_specs, check_vma=False
    )
```

profile of v0, /device:TPU:2, one launch (start us, length us, event | category | flops | bytes accessed | tf_op | source)
XLA Modules:
  0.0 2246.1 jit_solution(3896068341786399089)
XLA Ops:
  8.5 7.4 bitcast_multiply_fusion
  17.9 116.1 %all-reduce.22.cloned.1.call-done = f32[4,128,256]{2,1,0:T(8,128)} async-done(((f32[4,128,256]{2,1,0:T(8,128)}), f32[4,128,256]{2,1,0:T(8,128)}) %all-reduce.22.cloned.1.call-update) | async-done | bytes 524304 | tf_op jit(solution)/shard_map/psum | solution.py:36
  135.9 72.4 %all-reduce.24.cloned.1.call-done = f32[1,128,256]{2,1,0:T(8,128)} async-done(((f32[1,128,256]{2,1,0:T(8,128)}), f32[1,128,256]{2,1,0:T(8,128)}) %all-reduce.24.cloned.1.call-update) | async-done | bytes 131088 | tf_op jit(solution)/shard_map/psum | solution.py:11
  209.3 2.0 convolution_bitcast_fusion.5
  211.3 111.8 %all-reduce.26.cloned.1.call-done = f32[4,128,256]{2,1,0:T(8,128)} async-done(((f32[4,128,256]{2,1,0:T(8,128)}), f32[4,128,256]{2,1,0:T(8,128)}) %all-reduce.26.cloned.1.call-update) | async-done | bytes 524304 | tf_op jit(solution)/shard_map/psum | solution.py:36
  325.1 72.3 %all-reduce.28.cloned.1.call-done = f32[1,128,256]{2,1,0:T(8,128)} async-done(((f32[1,128,256]{2,1,0:T(8,128)}), f32[1,128,256]{2,1,0:T(8,128)}) %all-reduce.28.cloned.1.call-update) | async-done | bytes 131088 | tf_op jit(solution)/shard_map/psum | solution.py:11
  398.3 2.1 convolution_bitcast_fusion.4
  400.5 111.6 %all-reduce.30.cloned.1.call-done = f32[4,128,256]{2,1,0:T(8,128)} async-done(((f32[4,128,256]{2,1,0:T(8,128)}), f32[4,128,256]{2,1,0:T(8,128)}) %all-reduce.30.cloned.1.call-update) | async-done | bytes 524304 | tf_op jit(solution)/shard_map/psum | solution.py:36
  514.0 72.3 %all-reduce.32.cloned.1.call-done = f32[1,128,256]{2,1,0:T(8,128)} async-done(((f32[1,128,256]{2,1,0:T(8,128)}), f32[1,128,256]{2,1,0:T(8,128)}) %all-reduce.32.cloned.1.call-update) | async-done | bytes 131088 | tf_op jit(solution)/shard_map/psum | solution.py:11
  587.3 2.1 convolution_bitcast_fusion.3
  589.5 111.6 %all-reduce.34.cloned.1.call-done = f32[4,128,256]{2,1,0:T(8,128)} async-done(((f32[4,128,256]{2,1,0:T(8,128)}), f32[4,128,256]{2,1,0:T(8,128)}) %all-reduce.34.cloned.1.call-update) | async-done | bytes 524304 | tf_op jit(solution)/shard_map/psum | solution.py:36
  703.1 72.4 %all-reduce.36.cloned.1.call-done = f32[1,128,256]{2,1,0:T(8,128)} async-done(((f32[1,128,256]{2,1,0:T(8,128)}), f32[1,128,256]{2,1,0:T(8,128)}) %all-reduce.36.cloned.1.call-update) | async-done | bytes 131088 | tf_op jit(solution)/shard_map/psum | solution.py:11
  776.4 2.3 convolution_bitcast_fusion.2
  778.8 111.6 %all-reduce.38.cloned.1.call-done = f32[4,128,256]{2,1,0:T(8,128)} async-done(((f32[4,128,256]{2,1,0:T(8,128)}), f32[4,128,256]{2,1,0:T(8,128)}) %all-reduce.38.cloned.1.call-update) | async-done | bytes 524304 | tf_op jit(solution)/shard_map/psum | solution.py:36
  892.3 72.3 %all-reduce.40.cloned.1.call-done = f32[1,128,256]{2,1,0:T(8,128)} async-done(((f32[1,128,256]{2,1,0:T(8,128)}), f32[1,128,256]{2,1,0:T(8,128)}) %all-reduce.40.cloned.1.call-update) | async-done | bytes 131088 | tf_op jit(solution)/shard_map/psum | solution.py:11
  965.6 2.3 convolution_bitcast_fusion.1
  967.9 111.7 %all-reduce.42.cloned.1.call-done = f32[4,128,256]{2,1,0:T(8,128)} async-done(((f32[4,128,256]{2,1,0:T(8,128)}), f32[4,128,256]{2,1,0:T(8,128)}) %all-reduce.42.cloned.1.call-update) | async-done | bytes 524304 | tf_op jit(solution)/shard_map/psum | solution.py:36
  1081.5 72.3 %all-reduce.44.cloned.1.call-done = f32[1,128,256]{2,1,0:T(8,128)} async-done(((f32[1,128,256]{2,1,0:T(8,128)}), f32[1,128,256]{2,1,0:T(8,128)}) %all-reduce.44.cloned.1.call-update) | async-done | bytes 131088 | tf_op jit(solution)/shard_map/psum | solution.py:11
  1154.8 2.4 convolution_bitcast_fusion
  1157.2 111.7 %all-reduce.46.cloned.1.call-done = f32[4,128,256]{2,1,0:T(8,128)} async-done(((f32[4,128,256]{2,1,0:T(8,128)}), f32[4,128,256]{2,1,0:T(8,128)}) %all-reduce.46.cloned.1.call-update) | async-done | bytes 524304 | tf_op jit(solution)/shard_map/psum | solution.py:36
  1270.8 72.3 %all-reduce.48.cloned.1.call-done = f32[128,256]{1,0:T(8,128)} async-done(((f32[128,256]{1,0:T(8,128)}), f32[128,256]{1,0:T(8,128)}) %all-reduce.48.cloned.1.call-update) | async-done | bytes 131088 | tf_op jit(solution)/shard_map/psum | solution.py:11
  1345.2 48.3 %all-gather.15.cloned.1.call-done = bf16[4096,256]{0,1:T(8,128)(2,1)} async-done(((bf16[128,256]{0,1:T(8,128)(2,1)}), bf16[4096,256]{0,1:T(8,128)(2,1)}) %all-gather.15.cloned.1.call-update) | async-done | bytes 2097168 | tf_op jit(solution)/shard_map/all_gather | solution.py:72
  1393.4 2.1 copy.59
  1398.4 71.8 %all-reduce.50.cloned.1.call-done = f32[1,128,256]{2,1,0:T(8,128)} async-done(((f32[1,128,256]{2,1,0:T(8,128)}), f32[1,128,256]{2,1,0:T(8,128)}) %all-reduce.50.cloned.1.call-update) | async-done | bytes 131088 | tf_op jit(solution)/shard_map/psum | solution.py:67
  1472.2 48.6 %all-gather.17.cloned.1.call-done = bf16[4096,256]{0,1:T(8,128)(2,1)} async-done(((bf16[128,256]{0,1:T(8,128)(2,1)}), bf16[4096,256]{0,1:T(8,128)(2,1)}) %all-gather.17.cloned.1.call-update) | async-done | bytes 2097168 | tf_op jit(solution)/shard_map/all_gather | solution.py:72
  1520.8 2.1 copy.60
  1525.9 71.8 %all-reduce.52.cloned.1.call-done = f32[1,128,256]{2,1,0:T(8,128)} async-done(((f32[1,128,256]{2,1,0:T(8,128)}), f32[1,128,256]{2,1,0:T(8,128)}) %all-reduce.52.cloned.1.call-update) | async-done | bytes 131088 | tf_op jit(solution)/shard_map/psum | solution.py:67
  1599.6 48.4 %all-gather.19.cloned.1.call-done = bf16[4096,256]{0,1:T(8,128)(2,1)} async-done(((bf16[128,256]{0,1:T(8,128)(2,1)}), bf16[4096,256]{0,1:T(8,128)(2,1)}) %all-gather.19.cloned.1.call-update) | async-done | bytes 2097168 | tf_op jit(solution)/shard_map/all_gather | solution.py:72
  1648.1 2.1 copy.61
  1651.2 2.0 convolution_bitcast_fusion.11
  1653.2 71.8 %all-reduce.54.cloned.1.call-done = f32[1,128,256]{2,1,0:T(8,128)} async-done(((f32[1,128,256]{2,1,0:T(8,128)}), f32[1,128,256]{2,1,0:T(8,128)}) %all-reduce.54.cloned.1.call-update) | async-done | bytes 131088 | tf_op jit(solution)/shard_map/psum | solution.py:67
  1727.2 48.6 %all-gather.21.cloned.1.call-done = bf16[4096,256]{0,1:T(8,128)(2,1)} async-done(((bf16[128,256]{0,1:T(8,128)(2,1)}), bf16[4096,256]{0,1:T(8,128)(2,1)}) %all-gather.21.cloned.1.call-update) | async-done | bytes 2097168 | tf_op jit(solution)/shard_map/all_gather | solution.py:72
  1775.8 2.1 copy.62
  1778.9 2.1 convolution_bitcast_fusion.13
  1781.1 71.8 %all-reduce.56.cloned.1.call-done = f32[1,128,256]{2,1,0:T(8,128)} async-done(((f32[1,128,256]{2,1,0:T(8,128)}), f32[1,128,256]{2,1,0:T(8,128)}) %all-reduce.56.cloned.1.call-update) | async-done | bytes 131088 | tf_op jit(solution)/shard_map/psum | solution.py:67
  1854.9 48.4 %all-gather.23.cloned.1.call-done = bf16[4096,256]{0,1:T(8,128)(2,1)} async-done(((bf16[128,256]{0,1:T(8,128)(2,1)}), bf16[4096,256]{0,1:T(8,128)(2,1)}) %all-gather.23.cloned.1.call-update) | async-done | bytes 2097168 | tf_op jit(solution)/shard_map/all_gather | solution.py:72
  1903.3 2.1 copy.63
  1906.5 2.1 convolution_bitcast_fusion.12
  1908.8 71.8 %all-reduce.58.cloned.1.call-done = f32[1,128,256]{2,1,0:T(8,128)} async-done(((f32[1,128,256]{2,1,0:T(8,128)}), f32[1,128,256]{2,1,0:T(8,128)}) %all-reduce.58.cloned.1.call-update) | async-done | bytes 131088 | tf_op jit(solution)/shard_map/psum | solution.py:67
  1980.5 2.0 bitcast_convert_fusion.1
  1982.6 48.7 %all-gather.25.cloned.1.call-done = bf16[4096,256]{0,1:T(8,128)(2,1)} async-done(((bf16[128,256]{0,1:T(8,128)(2,1)}), bf16[4096,256]{0,1:T(8,128)(2,1)}) %all-gather.25.cloned.1.call-update) | async-done | bytes 2097168 | tf_op jit(solution)/shard_map/all_gather | solution.py:72
  2031.3 2.1 copy.64
  2034.5 2.2 convolution_bitcast_fusion.7
  2036.8 71.8 %all-reduce.60.cloned.1.call-done = f32[1,128,256]{2,1,0:T(8,128)} async-done(((f32[1,128,256]{2,1,0:T(8,128)}), f32[1,128,256]{2,1,0:T(8,128)}) %all-reduce.60.cloned.1.call-update) | async-done | bytes 131088 | tf_op jit(solution)/shard_map/psum | solution.py:67
  2110.7 48.2 %all-gather.27.cloned.1.call-done = bf16[4096,256]{0,1:T(8,128)(2,1)} async-done(((bf16[128,256]{0,1:T(8,128)(2,1)}), bf16[4096,256]{0,1:T(8,128)(2,1)}) %all-gather.27.cloned.1.call-update) | async-done | bytes 2097168 | tf_op jit(solution)/shard_map/all_gather | solution.py:72
  2158.9 2.1 copy.65
  2162.2 2.4 convolution_bitcast_fusion.6
  2164.6 71.8 %all-reduce.62.cloned.1.call-done = f32[1,128,256]{2,1,0:T(8,128)} async-done(((f32[1,128,256]{2,1,0:T(8,128)}), f32[1,128,256]{2,1,0:T(8,128)}) %all-reduce.62.cloned.1.call-update) | async-done | bytes 131088 | tf_op jit(solution)/shard_map/psum | solution.py:67
  (149 shorter events, 49.5 us)
Async XLA Ops:
  6.5 127.4 %all-reduce.22.cloned.1.call-start = ((), (), s32[]{:S(2)}) async-start(), calls=%async_computation | async-start | bytes 1048576 | tf_op jit(solution)/shard_map/psum | solution.py:36
  8.4 125.5 %copy-start = (f32[8,1,128,128]{3,2,1,0:T(8,128)S(1)}, f32[8,1,128,128]{3,2,1,0:T(8,128)}, u32[]{:S(2)}) copy-start(f32[8,1,128,128]{3,2,1,0:T(8,128)} %param.7) | copy-start | bytes 1572868
  8.5 125.5 %copy-start.1 = (f32[8,1,128,256]{3,2,1,0:T(8,128)S(1)}, f32[8,1,128,256]{3,2,1,0:T(8,128)}, u32[]{:S(2)}) copy-start(f32[8,1,128,256]{3,2,1,0:T(8,128)} %param.6) | copy-start | bytes 3145732
  17.8 190.6 %all-reduce.24.cloned.1.call-start = ((), (), s32[]{:S(2)}) async-start(), calls=%async_computation.1 | async-start | bytes 262144 | tf_op jit(solution)/shard_map/psum | solution.py:11
  135.8 187.3 %all-reduce.26.cloned.1.call-start = ((), (), s32[]{:S(2)}) async-start(), calls=%async_computation.2 | async-start | bytes 1048576 | tf_op jit(solution)/shard_map/psum | solution.py:36
  211.3 186.1 %all-reduce.28.cloned.1.call-start = ((), (), s32[]{:S(2)}) async-start(), calls=%async_computation.3 | async-start | bytes 262144 | tf_op jit(solution)/shard_map/psum | solution.py:11
  325.0 187.1 %all-reduce.30.cloned.1.call-start = ((), (), s32[]{:S(2)}) async-start(), calls=%async_computation.4 | async-start | bytes 1048576 | tf_op jit(solution)/shard_map/psum | solution.py:36
  400.4 185.9 %all-reduce.32.cloned.1.call-start = ((), (), s32[]{:S(2)}) async-start(), calls=%async_computation.5 | async-start | bytes 262144 | tf_op jit(solution)/shard_map/psum | solution.py:11
  514.0 187.1 %all-reduce.34.cloned.1.call-start = ((), (), s32[]{:S(2)}) async-start(), calls=%async_computation.6 | async-start | bytes 1048576 | tf_op jit(solution)/shard_map/psum | solution.py:36
  589.4 186.1 %all-reduce.36.cloned.1.call-start = ((), (), s32[]{:S(2)}) async-start(), calls=%async_computation.7 | async-start | bytes 262144 | tf_op jit(solution)/shard_map/psum | solution.py:11
  703.0 187.4 %all-reduce.38.cloned.1.call-start = ((), (), s32[]{:S(2)}) async-start(), calls=%async_computation.8 | async-start | bytes 1048576 | tf_op jit(solution)/shard_map/psum | solution.py:36
  778.7 185.9 %all-reduce.40.cloned.1.call-start = ((), (), s32[]{:S(2)}) async-start(), calls=%async_computation.9 | async-start | bytes 262144 | tf_op jit(solution)/shard_map/psum | solution.py:11
  892.3 187.3 %all-reduce.42.cloned.1.call-start = ((), (), s32[]{:S(2)}) async-start(), calls=%async_computation.10 | async-start | bytes 1048576 | tf_op jit(solution)/shard_map/psum | solution.py:36
  967.9 186.0 %all-reduce.44.cloned.1.call-start = ((), (), s32[]{:S(2)}) async-start(), calls=%async_computation.11 | async-start | bytes 262144 | tf_op jit(solution)/shard_map/psum | solution.py:11
  1081.5 187.4 %all-reduce.46.cloned.1.call-start = ((), (), s32[]{:S(2)}) async-start(), calls=%async_computation.12 | async-start | bytes 1048576 | tf_op jit(solution)/shard_map/psum | solution.py:36
  1157.2 186.0 %all-reduce.48.cloned.1.call-start = ((), (), s32[]{:S(2)}) async-start(), calls=%async_computation.13 | async-start | bytes 262144 | tf_op jit(solution)/shard_map/psum | solution.py:11
  1270.8 122.7 %all-gather.15.cloned.1.call-start = ((), (), s32[]{:S(2)}) async-start(), calls=%async_computation.21 | async-start | bytes 2162688 | tf_op jit(solution)/shard_map/all_gather | solution.py:72
  1345.1 125.1 %all-reduce.50.cloned.1.call-start = ((), (), s32[]{:S(2)}) async-start(), calls=%async_computation.14 | async-start | bytes 262144 | tf_op jit(solution)/shard_map/psum | solution.py:67
  1395.5 74.7 %copy-start.9 = (f32[1,128,256]{2,1,0:T(8,128)S(1)}, f32[1,128,256]{2,1,0:T(8,128)}, u32[]{:S(2)}) copy-start(f32[1,128,256]{2,1,0:T(8,128)} %all-reduce.44.cloned.1.call-done) | copy-start | bytes 393220
  1398.4 122.4 %all-gather.17.cloned.1.call-start = ((), (), s32[]{:S(2)}) async-start(), calls=%async_computation.22 | async-start | bytes 2162688 | tf_op jit(solution)/shard_map/all_gather | solution.py:72
  1472.1 125.5 %all-reduce.52.cloned.1.call-start = ((), (), s32[]{:S(2)}) async-start(), calls=%async_computation.15 | async-start | bytes 262144 | tf_op jit(solution)/shard_map/psum | solution.py:67
  1522.9 74.8 %copy-start.6 = (f32[1,128,256]{2,1,0:T(8,128)S(1)}, f32[1,128,256]{2,1,0:T(8,128)}, u32[]{:S(2)}) copy-start(f32[1,128,256]{2,1,0:T(8,128)} %all-reduce.40.cloned.1.call-done) | copy-start | bytes 393220
  1525.8 122.3 %all-gather.19.cloned.1.call-start = ((), (), s32[]{:S(2)}) async-start(), calls=%async_computation.23 | async-start | bytes 2162688 | tf_op jit(solution)/shard_map/all_gather | solution.py:72
  1599.6 125.4 %all-reduce.54.cloned.1.call-start = ((), (), s32[]{:S(2)}) async-start(), calls=%async_computation.16 | async-start | bytes 262144 | tf_op jit(solution)/shard_map/psum | solution.py:67
  1650.7 74.3 %copy-start.5 = (f32[1,128,256]{2,1,0:T(8,128)S(1)}, f32[1,128,256]{2,1,0:T(8,128)}, u32[]{:S(2)}) copy-start(f32[1,128,256]{2,1,0:T(8,128)} %all-reduce.36.cloned.1.call-done) | copy-start | bytes 393220
  1653.2 122.6 %all-gather.21.cloned.1.call-start = ((), (), s32[]{:S(2)}) async-start(), calls=%async_computation.24 | async-start | bytes 2162688 | tf_op jit(solution)/shard_map/all_gather | solution.py:72
  1727.0 125.9 %all-reduce.56.cloned.1.call-start = ((), (), s32[]{:S(2)}) async-start(), calls=%async_computation.17 | async-start | bytes 262144 | tf_op jit(solution)/shard_map/psum | solution.py:67
  1778.9 74.0 %copy-start.4 = (f32[1,128,256]{2,1,0:T(8,128)S(1)}, f32[1,128,256]{2,1,0:T(8,128)}, u32[]{:S(2)}) copy-start(f32[1,128,256]{2,1,0:T(8,128)} %all-reduce.32.cloned.1.call-done) | copy-start | bytes 393220
  1781.0 122.3 %all-gather.23.cloned.1.call-start = ((), (), s32[]{:S(2)}) async-start(), calls=%async_computation.25 | async-start | bytes 2162688 | tf_op jit(solution)/shard_map/all_gather | solution.py:72
  1854.8 125.7 %all-reduce.58.cloned.1.call-start = ((), (), s32[]{:S(2)}) async-start(), calls=%async_computation.18 | async-start | bytes 262144 | tf_op jit(solution)/shard_map/psum | solution.py:67
  1906.5 74.1 %copy-start.3 = (f32[1,128,256]{2,1,0:T(8,128)S(1)}, f32[1,128,256]{2,1,0:T(8,128)}, u32[]{:S(2)}) copy-start(f32[1,128,256]{2,1,0:T(8,128)} %all-reduce.28.cloned.1.call-done) | copy-start | bytes 393220
  1908.7 122.6 %all-gather.25.cloned.1.call-start = ((), (), s32[]{:S(2)}) async-start(), calls=%async_computation.26 | async-start | bytes 2162688 | tf_op jit(solution)/shard_map/all_gather | solution.py:72
  1982.5 126.1 %all-reduce.60.cloned.1.call-start = ((), (), s32[]{:S(2)}) async-start(), calls=%async_computation.19 | async-start | bytes 262144 | tf_op jit(solution)/shard_map/psum | solution.py:67
  2034.5 74.1 %copy-start.2 = (f32[1,128,256]{2,1,0:T(8,128)S(1)}, f32[1,128,256]{2,1,0:T(8,128)}, u32[]{:S(2)}) copy-start(f32[1,128,256]{2,1,0:T(8,128)} %all-reduce.24.cloned.1.call-done) | copy-start | bytes 393220
  2036.8 122.1 %all-gather.27.cloned.1.call-start = ((), (), s32[]{:S(2)}) async-start(), calls=%async_computation.27 | async-start | bytes 2162688 | tf_op jit(solution)/shard_map/all_gather | solution.py:72
  2110.6 125.8 %all-reduce.62.cloned.1.call-start = ((), (), s32[]{:S(2)}) async-start(), calls=%async_computation.20 | async-start | bytes 262144 | tf_op jit(solution)/shard_map/psum | solution.py:67
  2162.2 75.5 %copy-start.10 = (f32[256,128]{1,0:T(8,128)S(1)}, f32[256,128]{1,0:T(8,128)}, u32[]{:S(2)}) copy-start(f32[256,128]{1,0:T(8,128)} %get-tuple-element.39) | copy-start | bytes 393220
  2162.2 75.6 %copy-start.8 = (f32[256,128]{1,0:T(8,128)S(1)}, f32[256,128]{1,0:T(8,128)}, u32[]{:S(2)}) copy-start(f32[256,128]{1,0:T(8,128)} %get-tuple-element.37) | copy-start | bytes 393220
  2162.2 75.6 %copy-start.7 = (f32[256,128]{1,0:T(8,128)S(1)}, f32[256,128]{1,0:T(8,128)}, u32[]{:S(2)}) copy-start(f32[256,128]{1,0:T(8,128)} %get-tuple-element.35) | copy-start | bytes 393220
Sparse Core Ops, SparseCore 0:
  17.9 116.0 all-reduce.21
  136.4 71.9 all-reduce.23
  211.6 111.5 all-reduce.25
  325.4 71.9 all-reduce.27
  400.5 111.5 all-reduce.29
  514.4 71.9 all-reduce.31
  589.5 111.5 all-reduce.33
  703.5 71.9 all-reduce.35
  778.8 111.5 all-reduce.37
  892.7 71.9 all-reduce.39
  968.0 111.5 all-reduce.41
  1081.9 71.9 all-reduce.43
  1157.3 111.5 all-reduce.45
  1271.2 71.9 all-reduce.47
  1345.5 47.9 all-gather.14
  1398.5 71.6 all-reduce.49
  1472.8 47.9 all-gather.16
  1525.9 71.6 all-reduce.51
  1600.1 47.9 all-gather.18
  1653.3 71.6 all-reduce.53
  1727.8 47.9 all-gather.20
  1781.1 71.6 all-reduce.55
  1855.3 47.9 all-gather.22
  1908.8 71.6 all-reduce.57
  1983.3 47.9 all-gather.24
  2036.9 71.6 all-reduce.59
  2110.9 47.9 all-gather.26
  2164.7 71.6 all-reduce.61
where the time goes:
time: 2250 us
  waiting for transfers between devices  2130 us (95%)
  matrix products  58.4 us (3%)
  local copies, waits for them, and re-layouts  23.5 us (1%)
    psum x7, waiting for transfers between devices, per_device(): row_total = lax.psum(partial_sum, 'col')  786 us
    psum x7, waiting for transfers between devices, spread(): return lax.psum(kept, axis)  507 us
    psum x7, waiting for transfers between devices, per_device(): resid = resid - lax.psum(partial_sum, 'row')  502 us
    all_gather x7, waiting for transfers between devices, per_device(): pieces = lax.all_gather(low_solved[None], 'col', axis=0, tiled=True)  339 us
  transfers between devices with their start and end apart: 28, of which 28 were waited for; matrix products, arithmetic and copies ran while one was open for 0% of the time, Pallas kernels for 0%

commit v1 on v0

--- a/solution.py
+++ b/solution.py
@@ -4,11 +4,12 @@
 from jax.sharding import PartitionSpec as P
 
 LEVELS = 8
+drive_waves = lambda local, axis_name: lax.all_gather(local, axis_name=axis_name).sum(axis=0)
 
 
 def spread(value, axis, source):
     kept = jnp.where(lax.axis_index(axis) == source, value, 0).astype(value.dtype)
-    return lax.psum(kept, axis)
+    return drive_waves(kept, axis)
 
 
 def per_device(factor, pattern, loads, block_inverse):

time: 2250 us -> 2030 us (0.902)
  waiting for transfers between devices: 2130 us -> 1910 us
    psum x7 -> x0, waiting for transfers between devices: 507 us -> none  [spread(): return lax.psum(kept, axis)]
    all_gather x0 -> x7, waiting for transfers between devices: none -> 276 us  [lax.all_gather(local, axis_name=axis_name).sum(axis=0)]
where the time goes in v1:
time: 2030 us
  waiting for transfers between devices  1910 us (94%)
  matrix products  58.3 us (3%)
  local copies, waits for them, and re-layouts  36.4 us (2%)
    psum x7, waiting for transfers between devices, per_device(): row_total = lax.psum(partial_sum, 'col')  790 us
    psum x7, waiting for transfers between devices, per_device(): resid = resid - lax.psum(partial_sum, 'row')  502 us
    all_gather x7, waiting for transfers between devices, per_device(): pieces = lax.all_gather(low_solved[None], 'col', axis=0, tiled=True)  340 us
    all_gather x7, waiting for transfers between devices, lax.all_gather(local, axis_name=axis_name).sum(axis=0)  276 us
  transfers between devices with their start and end apart: 28, of which 28 were waited for; matrix products, arithmetic and copies ran while one was open for 0% of the time, Pallas kernels for 0%

profile of v1, /device:TPU:2, one launch (start us, length us, event | category | flops | bytes accessed | tf_op | source)
XLA Modules:
  0.0 2029.9 jit_solution(16727765825174284800)
XLA Ops:
  8.5 7.4 bitcast_multiply_fusion
  17.9 116.1 %all-reduce.15.cloned.1.call-done = f32[4,128,256]{2,1,0:T(8,128)} async-done(((f32[4,128,256]{2,1,0:T(8,128)}), f32[4,128,256]{2,1,0:T(8,128)}) %all-reduce.15.cloned.1.call-update) | async-done | bytes 524304 | tf_op jit(solution)/shard_map/psum | solution.py:37
  136.0 39.8 %all-gather.29.cloned.1.call-done = f32[1024,256]{0,1:T(8,128)} async-done(((f32[128,256]{0,1:T(8,128)}), f32[1024,256]{0,1:T(8,128)}) %all-gather.29.cloned.1.call-update) | async-done | bytes 1048592 | tf_op jit(solution)/shard_map/all_gather | solution.py:7
  177.6 2.0 convolution_bitcast_fusion.5
  179.6 112.4 %all-reduce.17.cloned.1.call-done = f32[4,128,256]{2,1,0:T(8,128)} async-done(((f32[4,128,256]{2,1,0:T(8,128)}), f32[4,128,256]{2,1,0:T(8,128)}) %all-reduce.17.cloned.1.call-update) | async-done | bytes 524304 | tf_op jit(solution)/shard_map/psum | solution.py:37
  294.0 39.8 %all-gather.31.cloned.1.call-done = f32[1024,256]{0,1:T(8,128)} async-done(((f32[128,256]{0,1:T(8,128)}), f32[1024,256]{0,1:T(8,128)}) %all-gather.31.cloned.1.call-update) | async-done | bytes 1048592 | tf_op jit(solution)/shard_map/all_gather | solution.py:7
  335.6 2.1 convolution_bitcast_fusion.4
  337.7 112.4 %all-reduce.19.cloned.1.call-done = f32[4,128,256]{2,1,0:T(8,128)} async-done(((f32[4,128,256]{2,1,0:T(8,128)}), f32[4,128,256]{2,1,0:T(8,128)}) %all-reduce.19.cloned.1.call-update) | async-done | bytes 524304 | tf_op jit(solution)/shard_map/psum | solution.py:37
  452.1 39.8 %all-gather.33.cloned.1.call-done = f32[1024,256]{0,1:T(8,128)} async-done(((f32[128,256]{0,1:T(8,128)}), f32[1024,256]{0,1:T(8,128)}) %all-gather.33.cloned.1.call-update) | async-done | bytes 1048592 | tf_op jit(solution)/shard_map/all_gather | solution.py:7
  493.7 2.1 convolution_bitcast_fusion.3
  495.9 112.4 %all-reduce.21.cloned.1.call-done = f32[4,128,256]{2,1,0:T(8,128)} async-done(((f32[4,128,256]{2,1,0:T(8,128)}), f32[4,128,256]{2,1,0:T(8,128)}) %all-reduce.21.cloned.1.call-update) | async-done | bytes 524304 | tf_op jit(solution)/shard_map/psum | solution.py:37
  612.8 37.2 %all-gather.35.cloned.1.call-done = f32[1024,256]{0,1:T(8,128)} async-done(((f32[128,256]{0,1:T(8,128)}), f32[1024,256]{0,1:T(8,128)}) %all-gather.35.cloned.1.call-update) | async-done | bytes 1048592 | tf_op jit(solution)/shard_map/all_gather | solution.py:7
  652.5 2.3 convolution_bitcast_fusion.2
  654.9 112.4 %all-reduce.23.cloned.1.call-done = f32[4,128,256]{2,1,0:T(8,128)} async-done(((f32[4,128,256]{2,1,0:T(8,128)}), f32[4,128,256]{2,1,0:T(8,128)}) %all-reduce.23.cloned.1.call-update) | async-done | bytes 524304 | tf_op jit(solution)/shard_map/psum | solution.py:37
  769.3 39.8 %all-gather.37.cloned.1.call-done = f32[1024,256]{0,1:T(8,128)} async-done(((f32[128,256]{0,1:T(8,128)}), f32[1024,256]{0,1:T(8,128)}) %all-gather.37.cloned.1.call-update) | async-done | bytes 1048592 | tf_op jit(solution)/shard_map/all_gather | solution.py:7
  810.9 2.3 convolution_bitcast_fusion.1
  813.3 112.4 %all-reduce.25.cloned.1.call-done = f32[4,128,256]{2,1,0:T(8,128)} async-done(((f32[4,128,256]{2,1,0:T(8,128)}), f32[4,128,256]{2,1,0:T(8,128)}) %all-reduce.25.cloned.1.call-update) | async-done | bytes 524304 | tf_op jit(solution)/shard_map/psum | solution.py:37
  927.6 39.8 %all-gather.39.cloned.1.call-done = f32[1024,256]{0,1:T(8,128)} async-done(((f32[128,256]{0,1:T(8,128)}), f32[1024,256]{0,1:T(8,128)}) %all-gather.39.cloned.1.call-update) | async-done | bytes 1048592 | tf_op jit(solution)/shard_map/all_gather | solution.py:7
  969.2 2.4 convolution_bitcast_fusion
  971.7 112.4 %all-reduce.27.cloned.1.call-done = f32[4,128,256]{2,1,0:T(8,128)} async-done(((f32[4,128,256]{2,1,0:T(8,128)}), f32[4,128,256]{2,1,0:T(8,128)}) %all-reduce.27.cloned.1.call-update) | async-done | bytes 524304 | tf_op jit(solution)/shard_map/psum | solution.py:37
  1086.1 39.8 %all-gather.41.cloned.1.call-done = f32[1024,256]{0,1:T(8,128)} async-done(((f32[128,256]{0,1:T(8,128)}), f32[1024,256]{0,1:T(8,128)}) %all-gather.41.cloned.1.call-update) | async-done | bytes 1048592 | tf_op jit(solution)/shard_map/all_gather | solution.py:7
  1128.5 48.7 %all-gather.43.cloned.1.call-done = bf16[4096,256]{0,1:T(8,128)(2,1)} async-done(((bf16[128,256]{0,1:T(8,128)(2,1)}), bf16[4096,256]{0,1:T(8,128)(2,1)}) %all-gather.43.cloned.1.call-update) | async-done | bytes 2097168 | tf_op jit(solution)/shard_map/all_gather | solution.py:73
  1177.3 2.1 copy.82
  1182.2 71.8 %all-reduce.29.cloned.1.call-done = f32[1,128,256]{2,1,0:T(8,128)} async-done(((f32[1,128,256]{2,1,0:T(8,128)}), f32[1,128,256]{2,1,0:T(8,128)}) %all-reduce.29.cloned.1.call-update) | async-done | bytes 131088 | tf_op jit(solution)/shard_map/psum | solution.py:68
  1256.2 48.1 %all-gather.45.cloned.1.call-done = bf16[4096,256]{0,1:T(8,128)(2,1)} async-done(((bf16[128,256]{0,1:T(8,128)(2,1)}), bf16[4096,256]{0,1:T(8,128)(2,1)}) %all-gather.45.cloned.1.call-update) | async-done | bytes 2097168 | tf_op jit(solution)/shard_map/all_gather | solution.py:73
  1304.3 2.1 copy.83
  1309.4 71.8 %all-reduce.31.cloned.1.call-done = f32[1,128,256]{2,1,0:T(8,128)} async-done(((f32[1,128,256]{2,1,0:T(8,128)}), f32[1,128,256]{2,1,0:T(8,128)}) %all-reduce.31.cloned.1.call-update) | async-done | bytes 131088 | tf_op jit(solution)/shard_map/psum | solution.py:68
  1383.1 48.7 %all-gather.47.cloned.1.call-done = bf16[4096,256]{0,1:T(8,128)(2,1)} async-done(((bf16[128,256]{0,1:T(8,128)(2,1)}), bf16[4096,256]{0,1:T(8,128)(2,1)}) %all-gather.47.cloned.1.call-update) | async-done | bytes 2097168 | tf_op jit(solution)/shard_map/all_gather | solution.py:73
  1431.9 2.1 copy.84
  1435.0 2.0 convolution_bitcast_fusion.11
  1437.0 71.8 %all-reduce.33.cloned.1.call-done = f32[1,128,256]{2,1,0:T(8,128)} async-done(((f32[1,128,256]{2,1,0:T(8,128)}), f32[1,128,256]{2,1,0:T(8,128)}) %all-reduce.33.cloned.1.call-update) | async-done | bytes 131088 | tf_op jit(solution)/shard_map/psum | solution.py:68
  1510.8 48.4 %all-gather.49.cloned.1.call-done = bf16[4096,256]{0,1:T(8,128)(2,1)} async-done(((bf16[128,256]{0,1:T(8,128)(2,1)}), bf16[4096,256]{0,1:T(8,128)(2,1)}) %all-gather.49.cloned.1.call-update) | async-done | bytes 2097168 | tf_op jit(solution)/shard_map/all_gather | solution.py:73
  1559.2 2.1 copy.85
  1562.4 2.1 convolution_bitcast_fusion.13
  1564.5 71.8 %all-reduce.35.cloned.1.call-done = f32[1,128,256]{2,1,0:T(8,128)} async-done(((f32[1,128,256]{2,1,0:T(8,128)}), f32[1,128,256]{2,1,0:T(8,128)}) %all-reduce.35.cloned.1.call-update) | async-done | bytes 131088 | tf_op jit(solution)/shard_map/psum | solution.py:68
  1638.3 48.7 %all-gather.51.cloned.1.call-done = bf16[4096,256]{0,1:T(8,128)(2,1)} async-done(((bf16[128,256]{0,1:T(8,128)(2,1)}), bf16[4096,256]{0,1:T(8,128)(2,1)}) %all-gather.51.cloned.1.call-update) | async-done | bytes 2097168 | tf_op jit(solution)/shard_map/all_gather | solution.py:73
  1687.0 2.1 copy.86
  1690.3 2.2 convolution_bitcast_fusion.12
  1692.5 71.8 %all-reduce.37.cloned.1.call-done = f32[1,128,256]{2,1,0:T(8,128)} async-done(((f32[1,128,256]{2,1,0:T(8,128)}), f32[1,128,256]{2,1,0:T(8,128)}) %all-reduce.37.cloned.1.call-update) | async-done | bytes 131088 | tf_op jit(solution)/shard_map/psum | solution.py:68
  1766.3 48.4 %all-gather.53.cloned.1.call-done = bf16[4096,256]{0,1:T(8,128)(2,1)} async-done(((bf16[128,256]{0,1:T(8,128)(2,1)}), bf16[4096,256]{0,1:T(8,128)(2,1)}) %all-gather.53.cloned.1.call-update) | async-done | bytes 2097168 | tf_op jit(solution)/shard_map/all_gather | solution.py:73
  1814.7 2.1 copy.87
  1818.0 2.2 convolution_bitcast_fusion.7
  1820.3 71.8 %all-reduce.39.cloned.1.call-done = f32[1,128,256]{2,1,0:T(8,128)} async-done(((f32[1,128,256]{2,1,0:T(8,128)}), f32[1,128,256]{2,1,0:T(8,128)}) %all-reduce.39.cloned.1.call-update) | async-done | bytes 131088 | tf_op jit(solution)/shard_map/psum | solution.py:68
  1892.1 2.0 bitcast_convert_fusion
  1894.1 48.6 %all-gather.55.cloned.1.call-done = bf16[4096,256]{0,1:T(8,128)(2,1)} async-done(((bf16[128,256]{0,1:T(8,128)(2,1)}), bf16[4096,256]{0,1:T(8,128)(2,1)}) %all-gather.55.cloned.1.call-update) | async-done | bytes 2097168 | tf_op jit(solution)/shard_map/all_gather | solution.py:73
  1942.7 2.1 copy.88
  1946.0 2.4 convolution_bitcast_fusion.6
  1948.4 71.8 %all-reduce.41.cloned.1.call-done = f32[1,128,256]{2,1,0:T(8,128)} async-done(((f32[1,128,256]{2,1,0:T(8,128)}), f32[1,128,256]{2,1,0:T(8,128)}) %all-reduce.41.cloned.1.call-update) | async-done | bytes 131088 | tf_op jit(solution)/shard_map/psum | solution.py:68
  (159 shorter events, 59.3 us)
Async XLA Ops:
  6.5 127.4 %all-reduce.15.cloned.1.call-start = ((), (), s32[]{:S(2)}) async-start(), calls=%async_computation | async-start | bytes 1048576 | tf_op jit(solution)/shard_map/psum | solution.py:37
  8.4 125.5 %copy-start = (f32[8,1,128,128]{3,2,1,0:T(8,128)S(1)}, f32[8,1,128,128]{3,2,1,0:T(8,128)}, u32[]{:S(2)}) copy-start(f32[8,1,128,128]{3,2,1,0:T(8,128)} %param.7) | copy-start | bytes 1572868
  8.5 125.5 %copy-start.1 = (f32[8,1,128,256]{3,2,1,0:T(8,128)S(1)}, f32[8,1,128,256]{3,2,1,0:T(8,128)}, u32[]{:S(2)}) copy-start(f32[8,1,128,256]{3,2,1,0:T(8,128)} %param.6) | copy-start | bytes 3145732
  17.8 158.0 %all-gather.29.cloned.1.call-start = ((), (), s32[]{:S(2)}) async-start(), calls=%async_computation.14 | async-start | bytes 1179648 | tf_op jit(solution)/shard_map/all_gather | solution.py:7
  135.9 156.0 %all-reduce.17.cloned.1.call-start = ((), (), s32[]{:S(2)}) async-start(), calls=%async_computation.1 | async-start | bytes 1048576 | tf_op jit(solution)/shard_map/psum | solution.py:37
  179.6 154.2 %all-gather.31.cloned.1.call-start = ((), (), s32[]{:S(2)}) async-start(), calls=%async_computation.15 | async-start | bytes 1179648 | tf_op jit(solution)/shard_map/all_gather | solution.py:7
  293.9 156.2 %all-reduce.19.cloned.1.call-start = ((), (), s32[]{:S(2)}) async-start(), calls=%async_computation.2 | async-start | bytes 1048576 | tf_op jit(solution)/shard_map/psum | solution.py:37
  337.7 154.2 %all-gather.33.cloned.1.call-start = ((), (), s32[]{:S(2)}) async-start(), calls=%async_computation.16 | async-start | bytes 1179648 | tf_op jit(solution)/shard_map/all_gather | solution.py:7
  452.1 156.2 %all-reduce.21.cloned.1.call-start = ((), (), s32[]{:S(2)}) async-start(), calls=%async_computation.3 | async-start | bytes 1048576 | tf_op jit(solution)/shard_map/psum | solution.py:37
  495.9 154.2 %all-gather.35.cloned.1.call-start = ((), (), s32[]{:S(2)}) async-start(), calls=%async_computation.17 | async-start | bytes 1179648 | tf_op jit(solution)/shard_map/all_gather | solution.py:7
  610.3 157.0 %all-reduce.23.cloned.1.call-start = ((), (), s32[]{:S(2)}) async-start(), calls=%async_computation.4 | async-start | bytes 1048576 | tf_op jit(solution)/shard_map/psum | solution.py:37
  654.9 154.2 %all-gather.37.cloned.1.call-start = ((), (), s32[]{:S(2)}) async-start(), calls=%async_computation.18 | async-start | bytes 1179648 | tf_op jit(solution)/shard_map/all_gather | solution.py:7
  769.2 156.4 %all-reduce.25.cloned.1.call-start = ((), (), s32[]{:S(2)}) async-start(), calls=%async_computation.5 | async-start | bytes 1048576 | tf_op jit(solution)/shard_map/psum | solution.py:37
  813.2 154.2 %all-gather.39.cloned.1.call-start = ((), (), s32[]{:S(2)}) async-start(), calls=%async_computation.19 | async-start | bytes 1179648 | tf_op jit(solution)/shard_map/all_gather | solution.py:7
  927.6 156.5 %all-reduce.27.cloned.1.call-start = ((), (), s32[]{:S(2)}) async-start(), calls=%async_computation.6 | async-start | bytes 1048576 | tf_op jit(solution)/shard_map/psum | solution.py:37
  971.7 154.2 %all-gather.41.cloned.1.call-start = ((), (), s32[]{:S(2)}) async-start(), calls=%async_computation.20 | async-start | bytes 1179648 | tf_op jit(solution)/shard_map/all_gather | solution.py:7
  1086.1 91.2 %all-gather.43.cloned.1.call-start = ((), (), s32[]{:S(2)}) async-start(), calls=%async_computation.21 | async-start | bytes 2162688 | tf_op jit(solution)/shard_map/all_gather | solution.py:73
  1128.5 125.5 %all-reduce.29.cloned.1.call-start = ((), (), s32[]{:S(2)}) async-start(), calls=%async_computation.7 | async-start | bytes 262144 | tf_op jit(solution)/shard_map/psum | solution.py:68
  1182.2 122.1 %all-gather.45.cloned.1.call-start = ((), (), s32[]{:S(2)}) async-start(), calls=%async_computation.22 | async-start | bytes 2162688 | tf_op jit(solution)/shard_map/all_gather | solution.py:73
  1256.0 125.2 %all-reduce.31.cloned.1.call-start = ((), (), s32[]{:S(2)}) async-start(), calls=%async_computation.8 | async-start | bytes 262144 | tf_op jit(solution)/shard_map/psum | solution.py:68
  1309.3 122.6 %all-gather.47.cloned.1.call-start = ((), (), s32[]{:S(2)}) async-start(), calls=%async_computation.23 | async-start | bytes 2162688 | tf_op jit(solution)/shard_map/all_gather | solution.py:73
  1383.1 125.7 %all-reduce.33.cloned.1.call-start = ((), (), s32[]{:S(2)}) async-start(), calls=%async_computation.9 | async-start | bytes 262144 | tf_op jit(solution)/shard_map/psum | solution.py:68
  1437.0 122.3 %all-gather.49.cloned.1.call-start = ((), (), s32[]{:S(2)}) async-start(), calls=%async_computation.24 | async-start | bytes 2162688 | tf_op jit(solution)/shard_map/all_gather | solution.py:73
  1510.8 125.5 %all-reduce.35.cloned.1.call-start = ((), (), s32[]{:S(2)}) async-start(), calls=%async_computation.10 | async-start | bytes 262144 | tf_op jit(solution)/shard_map/psum | solution.py:68
  1564.5 122.6 %all-gather.51.cloned.1.call-start = ((), (), s32[]{:S(2)}) async-start(), calls=%async_computation.25 | async-start | bytes 2162688 | tf_op jit(solution)/shard_map/all_gather | solution.py:73
  1638.3 126.0 %all-reduce.37.cloned.1.call-start = ((), (), s32[]{:S(2)}) async-start(), calls=%async_computation.11 | async-start | bytes 262144 | tf_op jit(solution)/shard_map/psum | solution.py:68
  1692.5 122.3 %all-gather.53.cloned.1.call-start = ((), (), s32[]{:S(2)}) async-start(), calls=%async_computation.26 | async-start | bytes 2162688 | tf_op jit(solution)/shard_map/all_gather | solution.py:73
  1766.3 125.8 %all-reduce.39.cloned.1.call-start = ((), (), s32[]{:S(2)}) async-start(), calls=%async_computation.12 | async-start | bytes 262144 | tf_op jit(solution)/shard_map/psum | solution.py:68
  1820.3 122.4 %all-gather.55.cloned.1.call-start = ((), (), s32[]{:S(2)}) async-start(), calls=%async_computation.27 | async-start | bytes 2162688 | tf_op jit(solution)/shard_map/all_gather | solution.py:73
  1894.1 126.2 %all-reduce.41.cloned.1.call-start = ((), (), s32[]{:S(2)}) async-start(), calls=%async_computation.13 | async-start | bytes 262144 | tf_op jit(solution)/shard_map/psum | solution.py:68
  1946.0 75.6 %copy-start.5 = (f32[256,128]{1,0:T(8,128)S(1)}, f32[256,128]{1,0:T(8,128)}, u32[]{:S(2)}) copy-start(f32[256,128]{1,0:T(8,128)} %get-tuple-element.39) | copy-start | bytes 393220
  1946.0 75.6 %copy-start.4 = (f32[256,128]{1,0:T(8,128)S(1)}, f32[256,128]{1,0:T(8,128)}, u32[]{:S(2)}) copy-start(f32[256,128]{1,0:T(8,128)} %get-tuple-element.37) | copy-start | bytes 393220
  1946.0 75.6 %copy-start.3 = (f32[256,128]{1,0:T(8,128)S(1)}, f32[256,128]{1,0:T(8,128)}, u32[]{:S(2)}) copy-start(f32[256,128]{1,0:T(8,128)} %get-tuple-element.35) | copy-start | bytes 393220
  1946.0 75.6 %copy-start.2 = (f32[256,128]{1,0:T(8,128)S(1)}, f32[256,128]{1,0:T(8,128)}, u32[]{:S(2)}) copy-start(f32[256,128]{1,0:T(8,128)} %get-tuple-element.33) | copy-start | bytes 393220
Sparse Core Ops, SparseCore 0:
  17.9 116.0 all-reduce.14
  136.1 39.6 all-gather.28
  179.7 112.2 all-reduce.16
  294.1 39.6 all-gather.30
  337.8 112.2 all-reduce.18
  452.2 39.6 all-gather.32
  496.0 112.2 all-reduce.20
  610.4 39.6 all-gather.34
  655.0 112.2 all-reduce.22
  769.4 39.6 all-gather.36
  813.3 112.2 all-reduce.24
  927.7 39.6 all-gather.38
  971.8 112.2 all-reduce.26
  1086.2 39.6 all-gather.40
  1128.6 48.6 all-gather.42
  1182.3 71.6 all-reduce.28
  1256.3 47.9 all-gather.44
  1309.4 71.6 all-reduce.30
  1383.9 47.9 all-gather.46
  1437.1 71.6 all-reduce.32
  1511.3 47.9 all-gather.48
  1564.6 71.6 all-reduce.34
  1639.1 47.9 all-gather.50
  1692.6 71.6 all-reduce.36
  1766.8 47.9 all-gather.52
  1820.4 71.6 all-reduce.38
  1894.7 47.9 all-gather.54
  1948.5 71.6 all-reduce.40
